TPU v7x, 32 devices: a whole 2x2x4 slice. The times are simulated.
32 devices in a mesh: groups: 2 (over y), seq: 16 (over z, x, core).
Axes of the slice: x: 2, y: 2, z: 4, core: 2. Of those that a mesh axis runs over, the one named last changes fastest.
Arguments:
- queries: bfloat16 [4096, 1536], P(('groups', 'seq')), parts along dimension 0, may hold values from -6 to 6
- keys: bfloat16 [4096, 1536], P(('groups', 'seq')), parts along dimension 0, may hold values from -6 to 6
- values: bfloat16 [4096, 1536], P(('groups', 'seq')), parts along dimension 0, may hold values from -6 to 6
- w_out: bfloat16 [1536, 3072], replicated, may hold values from -0.15625 to 0.15625
- shift_mod: float32 [6144], P('groups'), parts along dimension 0, may hold values from -5 to 5
- scale_mod: float32 [6144], P('groups'), parts along dimension 0, may hold values from -3 to 3
- w_final: bfloat16 [3072, 64], replicated, may hold values from -0.109375 to 0.109375
- conv_weight: bfloat16 [432, 512], replicated, may hold values from -0.3125 to 0.3125
- conv_bias: float32 [512], replicated, may hold values from -3 to 3
Outputs:
- decoded: bfloat16 [8, 32, 64, 512], P('groups', 'seq'), parts along dimension 0
There are 2 independent parts, one for each index of `groups`. A program takes and returns all parts, laid end to end along the dimension named above; an argument that names none is the same for every part. Nothing has to cross between parts.
All inputs are finite; a program needn't handle non-finite values.
Results may differ from a plain program's by a relative error of at most 0.018.
Values may be sent and summed in bfloat16 or wider, within the bound.
A program may use at most 192 MiB of HBM per device.

v0:
```python
import math

import jax
import jax.numpy as jnp
from jax import lax
from jax.sharding import PartitionSpec as P

HEADS = 12
HEAD_DIM = 128
HEAD_GROUPS = 4
LATENT_CH = 16
FRAMES = 4
ROWS = 32
COLS_DEV = 1


def with_halo(cells, sides, width):
    for axis, dim in sides:
        count = lax.axis_size(axis)
        ends = count - 1
        head = lax.slice_in_dim(cells, 0, width, axis=dim)
        tail = lax.slice_in_dim(cells, cells.shape[dim] - width, cells.shape[dim], axis=dim)
        cells = jnp.concatenate(
            [
                lax.ppermute(tail, axis, [(i, (i + 1) % count) for i in range(ends)]),
                cells,
                lax.ppermute(head, axis, [((i + 1) % count, i) for i in range(ends)]),
            ],
            axis=dim,
        )
    return cells


def to_pieces(source, blocks):
    piece_rows = source.shape[0] // blocks
    grouped = source.reshape(blocks, piece_rows, HEAD_GROUPS, source.shape[1] // HEAD_GROUPS)
    return jnp.transpose(grouped, (0, 2, 1, 3)).reshape(
        blocks * HEAD_GROUPS, piece_rows, source.shape[1] // HEAD_GROUPS
    )


def absorb(state, key_part, value_part, query_rows):
    key_count = key_part.shape[0]
    block_rows = min(key_count, max(128, 1048576 // query_rows.shape[0]))
    per_head = HEADS // HEAD_GROUPS
    key_blocks = key_part.reshape(key_count // block_rows, block_rows, per_head, HEAD_DIM)
    value_blocks = value_part.reshape(key_count // block_rows, block_rows, per_head, HEAD_DIM)
    inv_root = 1.0 / math.sqrt(HEAD_DIM)

    def one_block(state_in, kv_block):
        run_max, run_sum, accumulated = state_in
        key_block, value_block = kv_block
        scores = (
            jnp.einsum("qhd,khd->hqk", query_rows, key_block, preferred_element_type=jnp.float32)
            * inv_root
        )
        new_max = jnp.maximum(run_max, jnp.max(scores, axis=2))
        factor = jnp.exp(run_max - new_max)
        exp_scores = jnp.exp(scores - new_max[:, :, None])
        run_sum = run_sum * factor + jnp.sum(exp_scores, axis=2)
        update = jnp.einsum(
            "hqk,khd->hqd",
            exp_scores.astype(jnp.bfloat16),
            value_block,
            preferred_element_type=jnp.float32,
        )
        accumulated = accumulated * factor[:, :, None] + update
        return ((new_max, run_sum, accumulated), None)

    state, unused = lax.scan(one_block, state, (key_blocks, value_blocks))
    return state


def fresh_state(per_head, count):
    return (
        jnp.full((per_head, count), -1e30, jnp.float32),
        jnp.zeros((per_head, count), jnp.float32),
        jnp.zeros((per_head, count, HEAD_DIM), jnp.float32),
    )


def convolve(padded, conv_weight, conv_bias, frames, width, height):
    taps = []
    for shift_t in range(3):
        for shift_x in range(3):
            for shift_y in range(3):
                taps.append(
                    padded[
                        shift_t : shift_t + frames,
                        shift_x : shift_x + width,
                        shift_y : shift_y + height,
                        :,
                    ]
                )
    stacked = jnp.concatenate(taps, axis=3)
    flat = stacked.reshape(frames * width * height, stacked.shape[3])
    output = jnp.dot(flat, conv_weight, preferred_element_type=jnp.float32) + conv_bias
    return output.astype(jnp.bfloat16).reshape(frames, width, height, conv_weight.shape[1])


def shards(queries, keys, values, w_out, shift_mod, scale_mod, w_final, conv_weight, conv_bias):
    devices = lax.axis_size("seq")
    position = lax.axis_index("seq")
    tok_dev = queries.shape[0]
    blocks = devices // HEAD_GROUPS
    per_head = HEADS // HEAD_GROUPS
    group_width = per_head * HEAD_DIM
    query_count = tok_dev * HEAD_GROUPS
    got_queries = lax.all_to_all(
        to_pieces(queries, blocks), "seq", split_axis=0, concat_axis=1, tiled=True
    )
    query_rows = got_queries.reshape(query_count, per_head, HEAD_DIM)
    key_groups = jnp.transpose(keys.reshape(tok_dev, HEAD_GROUPS, group_width), (1, 0, 2))
    value_groups = jnp.transpose(values.reshape(tok_dev, HEAD_GROUPS, group_width), (1, 0, 2))
    key_copies = jnp.broadcast_to(
        key_groups[None], (blocks, HEAD_GROUPS, tok_dev, group_width)
    ).reshape(devices, tok_dev, group_width)
    value_copies = jnp.broadcast_to(
        value_groups[None], (blocks, HEAD_GROUPS, tok_dev, group_width)
    ).reshape(devices, tok_dev, group_width)
    all_keys, all_values = (
        lax.all_to_all(key_copies, "seq", split_axis=0, concat_axis=1, tiled=True),
        lax.all_to_all(value_copies, "seq", split_axis=0, concat_axis=1, tiled=True),
    )
    state = absorb(fresh_state(per_head, query_count), all_keys[0], all_values[0], query_rows)
    run_max, run_sum, accumulated = state
    result = (accumulated / run_sum[:, :, None]).astype(jnp.bfloat16)
    result = jnp.transpose(result, (1, 0, 2)).reshape(1, query_count, group_width)
    returned = lax.all_to_all(result, "seq", split_axis=1, concat_axis=0, tiled=True)
    piece_rows = tok_dev // blocks
    attended = jnp.transpose(
        returned.reshape(blocks, HEAD_GROUPS, piece_rows, group_width), (0, 2, 1, 3)
    ).reshape(tok_dev, HEADS * HEAD_DIM)
    projected = jnp.dot(attended, w_out, preferred_element_type=jnp.float32)
    centered = projected - jnp.mean(projected, axis=1, keepdims=True)
    variance = jnp.mean(centered * centered, axis=1, keepdims=True)
    normed = (centered * lax.rsqrt(variance + 1e-06) * (1.0 + scale_mod) + shift_mod).astype(
        jnp.bfloat16
    )
    patches = jnp.dot(normed, w_final, preferred_element_type=jnp.float32).astype(jnp.bfloat16)
    rows_dev = FRAMES * ROWS // devices
    columns = COLS_DEV * devices
    laid = patches.reshape(rows_dev, columns, 4 * LATENT_CH)
    tile = lax.all_to_all(laid, "seq", split_axis=1, concat_axis=0, tiled=True)
    latent = tile.reshape(FRAMES, ROWS, COLS_DEV, LATENT_CH, 2, 2).transpose(0, 2, 5, 1, 4, 3)
    latent = latent.reshape(FRAMES, 2 * COLS_DEV, 2 * ROWS, LATENT_CH)
    rimmed = with_halo(latent, (("seq", 1),), 1)
    left_rim = jnp.where(position == 0, latent[:, :1], rimmed[:, :1])
    right_rim = jnp.where(position == devices - 1, latent[:, -1:], rimmed[:, -1:])
    widened = jnp.concatenate([left_rim, latent, right_rim], axis=1)
    padded = jnp.pad(widened, ((2, 0), (0, 0), (1, 1), (0, 0)), mode="edge")
    return convolve(padded, conv_weight, conv_bias, FRAMES, 2 * COLS_DEV, 2 * ROWS)


def solution(mesh):
    placed = (
        P(("groups", "seq"), None),
        P(("groups", "seq"), None),
        P(("groups", "seq"), None),
        P(),
        P("groups"),
        P("groups"),
        P(),
        P(),
        P(),
    )
    return jax.shard_map(
        shards,
        mesh=mesh,
        in_specs=placed,
        out_specs=P("groups", "seq", None, None),
        check_vma=False,
    )
```

profile of v0, /device:TPU:3, one launch (start us, length us, event | category | flops | bytes accessed | tf_op | source)
XLA Modules:
  0.0 180.4 jit_solution(2948887893393950316)
XLA Ops:
  0.0 1.2 reshape.125
  1.2 0.8 copy.31
  2.0 6.6 %all-to-all-start = ((bf16[16,32,384]{2,1,0:T(8,128)(2,1)}), bf16[16,32,384]{2,1,0:T(8,128)(2,1)S(1)}, u32[]{:S(2)}, u32[]{:S(2)}) async-start(bf16[16,32,384]{2,1,0:T(8,128)(2,1)} %bitcast.1), calls=%async_computation | async-start | bytes 786432 | tf_op jit(solution)/shard_map/all_to_all | solution.py:109
  8.7 0.3 copy.32
  9.0 10.7 %all-to-all-done = bf16[16,32,384]{2,1,0:T(8,128)(2,1)S(1)} async-done(((bf16[16,32,384]{2,1,0:T(8,128)(2,1)}), bf16[16,32,384]{2,1,0:T(8,128)(2,1)S(1)}, u32[]{:S(2)}, u32[]{:S(2)}) %all-to-all-start) | async-done | bytes 393248 | tf_op jit(solution)/shard_map/all_to_all | solution.py:109
  19.7 1.5 broadcast_in_dim.15
  21.2 4.8 %all-to-all-start.1 = ((bf16[16,128,384]{1,2,0:T(8,128)(2,1)}), bf16[16,128,384]{1,2,0:T(8,128)(2,1)S(1)}, u32[]{:S(2)}, u32[]{:S(2)}) async-start(bf16[16,128,384]{1,2,0:T(8,128)(2,1)} %bitcast.87), calls=%async_computation.1 | async-start | bytes 3145728 | tf_op jit(solution)/shard_map/all_to_all | solution.py:122
  26.1 0.3 copy.36
  26.4 33.1 %all-to-all-done.1 = bf16[16,128,384]{1,2,0:T(8,128)(2,1)S(1)} async-done(((bf16[16,128,384]{1,2,0:T(8,128)(2,1)}), bf16[16,128,384]{1,2,0:T(8,128)(2,1)S(1)}, u32[]{:S(2)}, u32[]{:S(2)}) %all-to-all-start.1) | async-done | bytes 1572896 | tf_op jit(solution)/shard_map/all_to_all | solution.py:122
  59.5 1.7 broadcast_in_dim.16
  61.2 7.5 %all-to-all-start.2 = ((bf16[16,128,384]{1,2,0:T(8,128)(2,1)}), bf16[16,128,384]{1,2,0:T(8,128)(2,1)S(1)}, u32[]{:S(2)}, u32[]{:S(2)}) async-start(bf16[16,128,384]{1,2,0:T(8,128)(2,1)} %bitcast.86), calls=%async_computation.2 | async-start | bytes 3145728 | tf_op jit(solution)/shard_map/all_to_all | solution.py:123
  68.8 3.6 %copy.33 = bf16[16,128,384]{1,0,2:T(8,128)(2,1)} copy(bf16[16,128,384]{1,2,0:T(8,128)(2,1)} %copy-done.2) | data formatting | bytes 3145728 | tf_op jit(solution)/shard_map/all_to_all | solution.py:122
  72.4 3.7 %squeeze.9 = bf16[2048,3,128]{0,2,1:T(8,128)(2,1)} reshape(bf16[16,128,384]{1,0,2:T(8,128)(2,1)} %copy.33) | data formatting | bytes 3145728 | tf_op jit(solution)/shard_map/while/body/jit(dynamic_index_in_dim)/squeeze | solution.py:70
  76.1 3.3 %multiply_reduce_fusion = (f32[3,512]{1,0:T(4,128)S(1)}, f32[3,512,2048]{2,1,0:T(8,128)S(1)}) fusion(bf16[2048,3,128]{0,2,1:T(8,128)(2,1)} %squeeze.9, bf16[512,3,128]{2,1,0:T(4,128)(2,1)S(1)} %reshape.127), kind=kOutput, calls=%fused_computation.1 | convolution fusion | flops 811596288 | bytes 14555136 | tf_op jit(solution)/shard_map/while/body/eval_jaxpr/qhd,khd->hqk/dot_general | solution.py:54
  79.4 2.5 %fusion = f32[3,512]{1,0:T(4,128)S(1)} fusion(f32[3,512,2048]{2,1,0:T(8,128)S(1)} %get-tuple-element.63, f32[3,512]{1,0:T(4,128)S(1)} %get-tuple-element.61), kind=kLoop, calls=%fused_computation.2 | loop fusion | flops 9435648 | bytes 12595200 | tf_op jit(solution)/shard_map/while/body/eval_jaxpr/reduce_sum | solution.py:60
  81.9 2.0 %copy-done.1 = f32[3,512,2048]{2,1,0:T(8,128)} copy-done((f32[3,512,2048]{2,1,0:T(8,128)}, f32[3,512,2048]{2,1,0:T(8,128)S(1)}, u32[]{:S(2)}) %copy-start.1) | copy-done | bytes 12582936
  83.9 18.2 %all-to-all-done.2 = bf16[16,128,384]{1,2,0:T(8,128)(2,1)S(1)} async-done(((bf16[16,128,384]{1,2,0:T(8,128)(2,1)}), bf16[16,128,384]{1,2,0:T(8,128)(2,1)S(1)}, u32[]{:S(2)}, u32[]{:S(2)}) %all-to-all-start.2) | async-done | bytes 1572896 | tf_op jit(solution)/shard_map/all_to_all | solution.py:123
  102.2 2.2 %copy.37 = bf16[16,128,384]{1,0,2:T(8,128)(2,1)} copy(bf16[16,128,384]{1,2,0:T(8,128)(2,1)S(1)} %all-to-all-done.2) | data formatting | bytes 3145728 | tf_op jit(solution)/shard_map/all_to_all | solution.py:123
  104.3 2.5 %squeeze.10 = bf16[2048,3,128]{0,2,1:T(8,128)(2,1)S(1)} reshape(bf16[16,128,384]{1,0,2:T(8,128)(2,1)} %copy.37) | data formatting | bytes 3145728 | tf_op jit(solution)/shard_map/while/body/jit(dynamic_index_in_dim)/squeeze | solution.py:70
  106.9 7.1 %fusion.16 = bf16[512,3,128]{0,2,1:T(8,128)(2,1)S(1)} fusion(bf16[2048,3,128]{0,2,1:T(8,128)(2,1)S(1)} %squeeze.10, f32[3,512,2048]{2,1,0:T(8,128)} %copy-done.1, f32[3,512]{1,0:T(4,128)S(1)} %get-tuple-element.61, f32[512,3]{0,1:T(4,128)S(1)} %bitcast_add_fusion, f32[512,3]{0,1:T(4,128)S(1)} %get-tuple-element.60), kind=kOutput, calls=%fused_computation.15 | convolution fusion | flops 815333376 | bytes 14567424 | tf_op jit(solution)/shard_map/while/body/eval_jaxpr/hqk,khd->hqd/dot_general | solution.py:61
  114.0 1.1 copy.38
  115.2 0.5 broadcast.84
  115.7 3.0 %reduce = bf16[512,384]{1,0:T(8,128)(2,1)S(1)} reduce(bf16[512,1,384]{2,1,0:T(2,128)(2,1)S(1)} %bitcast.92, bf16[]{:T(256)} %broadcast.84), dimensions={1}, to_apply=%bitcast.71.reduce_sub_computation | reduce | bytes 786434
  118.7 0.8 reshape.140
  119.5 7.5 %all-to-all-start.3 = ((bf16[16,2,6144]{2,1,0:T(2,128)(2,1)}), bf16[16,2,6144]{2,1,0:T(2,128)(2,1)S(1)}, u32[]{:S(2)}, u32[]{:S(2)}) async-start(bf16[16,2,6144]{2,1,0:T(2,128)(2,1)} %reshape.140), calls=%async_computation.3 | async-start | bytes 786432 | tf_op jit(solution)/shard_map/all_to_all | solution.py:129
  127.1 11.1 %all-to-all-done.3 = bf16[16,2,6144]{2,1,0:T(2,128)(2,1)S(1)} async-done(((bf16[16,2,6144]{2,1,0:T(2,128)(2,1)}), bf16[16,2,6144]{2,1,0:T(2,128)(2,1)S(1)}, u32[]{:S(2)}, u32[]{:S(2)}) %all-to-all-start.3) | async-done | bytes 393248 | tf_op jit(solution)/shard_map/all_to_all | solution.py:129
  138.2 0.4 reshape.141
  138.6 0.2 copy.39
  138.9 5.3 %fusion.31 = (f32[128]{0:T(128)S(1)}, f32[128,3072]{1,0:T(8,128)S(1)}) fusion(bf16[128,1536]{1,0:T(8,128)(2,1)S(1)} %bitcast.94, bf16[1536,3072]{1,0:T(8,128)(2,1)} %param.12), kind=kOutput, calls=%fused_computation.43 | convolution fusion | flops 1208352640 | bytes 11403776 | tf_op jit(solution)/shard_map/dot_general | solution.py:134
  144.2 0.3 multiply_reduce_fusion.1
  144.5 0.7 copy-done.7
  145.2 0.5 convolution_convert_fusion
  145.9 9.3 %all_to_all.51 = bf16[16,2,256]{2,1,0:T(2,128)(2,1)S(1)} all-to-all(bf16[16,2,256]{2,1,0:T(2,128)(2,1)S(1)} %reshape.142), channel_id=1, replica_groups=mesh['groups'=2,'seq'=16] {'seq'}, dimensions={0} | all-to-all | bytes 32768 | tf_op jit(solution)/shard_map/all_to_all | solution.py:144
  155.3 0.2 copy.42
  155.6 0.2 reshape.136
  155.7 0.1 copy.43
  155.9 3.4 %collective-permute-start = (bf16[4,1,64,16]{3,2,1,0:T(8,128)(2,1)S(1)}, bf16[4,1,64,16]{3,2,1,0:T(8,128)(2,1)S(1)}, u32[]{:S(2)}, u32[]{:S(2)}) collective-permute-start(bf16[4,1,64,16]{3,2,1,0:T(8,128)(2,1)S(1)} %get-tuple-element.19), channel_id=1, source_target_pairs={{0,1},{1,2},{2,3},{3,4},{4,5},{5,6},{6,7},{7,8},{8,9},{9,10},{10,1... | collective-permute-start | bytes 24584 | tf_op jit(solution)/shard_map/ppermute | solution.py:25
  159.3 1.9 %collective-permute-start.1 = (bf16[4,1,64,16]{3,2,1,0:T(8,128)(2,1)S(1)}, bf16[4,1,64,16]{3,2,1,0:T(8,128)(2,1)S(1)}, u32[]{:S(2)}, u32[]{:S(2)}) collective-permute-start(bf16[4,1,64,16]{3,2,1,0:T(8,128)(2,1)S(1)} %get-tuple-element.20), channel_id=1, source_target_pairs={{1,0},{2,1},{3,2},{4,3},{5,4},{6,5},{7,6},{8,7},{9,8},{10,9},{11,1... | collective-permute-start | bytes 24584 | tf_op jit(solution)/shard_map/ppermute | solution.py:27
  161.3 4.4 %collective-permute-done.1 = bf16[4,1,64,16]{3,2,1,0:T(8,128)(2,1)S(1)} collective-permute-done((bf16[4,1,64,16]{3,2,1,0:T(8,128)(2,1)S(1)}, bf16[4,1,64,16]{3,2,1,0:T(8,128)(2,1)S(1)}, u32[]{:S(2)}, u32[]{:S(2)}) %collective-permute-start.1) | collective-permute-done | bytes 8224 | tf_op jit(solution)/shard_map/ppermute | solution.py:27
  166.2 0.7 fusion.29
  166.9 0.1 copy.76
  167.1 0.1 pad_maximum_fusion
  167.2 0.2 fusion.27
  167.5 0.1 copy.49
  167.8 0.1 copy.52
  167.9 0.1 copy.53
  168.0 0.1 copy.55
  168.2 0.1 copy.56
  168.3 0.1 copy.58
  168.4 0.1 copy.59
  168.6 0.1 copy.61
  168.7 0.1 copy.62
  168.8 0.1 copy.64
  168.9 0.1 copy.65
  169.1 0.1 copy.69
  169.3 0.1 copy.72
  169.5 0.1 copy.73
  169.9 0.9 copy.51
  170.7 1.5 copy.54
  172.3 0.8 copy.57
  173.0 0.8 copy.60
  173.8 0.8 copy.63
  174.6 3.6 %concatenate.128 = bf16[512,432]{1,0:T(8,128)(2,1)} concatenate(bf16[512,16]{1,0:T(8,128)(2,1)S(1)} %bitcast.102, bf16[512,16]{1,0:T(8,128)(2,1)S(1)} %bitcast.120, bf16[512,16]{1,0:T(8,128)(2,1)S(1)} %bitcast.103, bf16[512,16]{1,0:T(8,128)(2,1)S(1)} %bitcast.104, bf16[512,16]{1,0:T(8,128)(2,1)S(1)} %bitcast.121, bf16[512,16]{1,0:T(8,128)(2,1)S(1)} %bitcast.105, ...), dimensions={1} | concatenate | bytes 884736 | tf_op jit(solution)/shard_map/concatenate | solution.py:95
  178.1 2.3 %fusion.9 = bf16[512,512]{1,0:T(8,128)(2,1)} fusion(bf16[512,432]{1,0:T(8,128)(2,1)} %concatenate.128, bf16[432,512]{1,0:T(8,128)(2,1)S(1)} %copy-done, f32[512]{0:T(512)S(1)} %copy-done.9), kind=kOutput, calls=%fused_computation.11 | convolution fusion | flops 227016704 | bytes 1411072 | tf_op jit(solution)/shard_map/dot_general | solution.py:97
  (50 shorter events, 2.0 us)
Async XLA Ops:
  0.0 178.1 %copy-start = (bf16[432,512]{1,0:T(8,128)(2,1)S(1)}, bf16[432,512]{1,0:T(8,128)(2,1)}, u32[]{:S(2)}) copy-start(bf16[432,512]{1,0:T(8,128)(2,1)} %param.16) | copy-start | bytes 1327108
  0.0 8.6 %copy-start.3 = (bf16[128,1536]{1,0:T(8,128)(2,1)S(1)}, bf16[128,1536]{1,0:T(8,128)(2,1)}, u32[]{:S(2)}) copy-start(bf16[128,1536]{1,0:T(8,128)(2,1)} %param.10) | copy-start | bytes 1179652
  2.0 17.8 %all-to-all-start = ((bf16[16,32,384]{2,1,0:T(8,128)(2,1)}), bf16[16,32,384]{2,1,0:T(8,128)(2,1)S(1)}, u32[]{:S(2)}, u32[]{:S(2)}) async-start(bf16[16,32,384]{2,1,0:T(8,128)(2,1)} %bitcast.1), calls=%async_computation | async-start | bytes 786432 | tf_op jit(solution)/shard_map/all_to_all | solution.py:109
  21.2 4.8 %copy-start.4 = (bf16[128,1536]{1,0:T(8,128)(2,1)S(1)}, bf16[128,1536]{1,0:T(8,128)(2,1)}, u32[]{:S(2)}) copy-start(bf16[128,1536]{1,0:T(8,128)(2,1)} %param.11) | copy-start | bytes 1179652
  21.2 38.2 %all-to-all-start.1 = ((bf16[16,128,384]{1,2,0:T(8,128)(2,1)}), bf16[16,128,384]{1,2,0:T(8,128)(2,1)S(1)}, u32[]{:S(2)}, u32[]{:S(2)}) async-start(bf16[16,128,384]{1,2,0:T(8,128)(2,1)} %bitcast.87), calls=%async_computation.1 | async-start | bytes 3145728 | tf_op jit(solution)/shard_map/all_to_all | solution.py:122
  59.5 1.7 copy-start.2
  61.2 40.9 %all-to-all-start.2 = ((bf16[16,128,384]{1,2,0:T(8,128)(2,1)}), bf16[16,128,384]{1,2,0:T(8,128)(2,1)S(1)}, u32[]{:S(2)}, u32[]{:S(2)}) async-start(bf16[16,128,384]{1,2,0:T(8,128)(2,1)} %bitcast.86), calls=%async_computation.2 | async-start | bytes 3145728 | tf_op jit(solution)/shard_map/all_to_all | solution.py:123
  79.4 4.5 %copy-start.1 = (f32[3,512,2048]{2,1,0:T(8,128)}, f32[3,512,2048]{2,1,0:T(8,128)S(1)}, u32[]{:S(2)}) copy-start(f32[3,512,2048]{2,1,0:T(8,128)S(1)} %get-tuple-element.63) | copy-start | bytes 37748740
  115.1 11.9 %copy-start.6 = (f32[3072]{0:T(1024)S(1)}, f32[3072]{0:T(1024)}, u32[]{:S(2)}) copy-start(f32[3072]{0:T(1024)} %param.14) | copy-start | bytes 36868
  119.5 18.7 %all-to-all-start.3 = ((bf16[16,2,6144]{2,1,0:T(2,128)(2,1)}), bf16[16,2,6144]{2,1,0:T(2,128)(2,1)S(1)}, u32[]{:S(2)}, u32[]{:S(2)}) async-start(bf16[16,2,6144]{2,1,0:T(2,128)(2,1)} %reshape.140), calls=%async_computation.3 | async-start | bytes 786432 | tf_op jit(solution)/shard_map/all_to_all | solution.py:129
  144.2 1.0 copy-start.7
  144.2 1.0 copy-start.8
  155.9 5.4 %collective-permute-start = (bf16[4,1,64,16]{3,2,1,0:T(8,128)(2,1)S(1)}, bf16[4,1,64,16]{3,2,1,0:T(8,128)(2,1)S(1)}, u32[]{:S(2)}, u32[]{:S(2)}) collective-permute-start(bf16[4,1,64,16]{3,2,1,0:T(8,128)(2,1)S(1)} %get-tuple-element.19), channel_id=1, source_target_pairs={{0,1},{1,2},{2,3},{3,4},{4,5},{5,6},{6,7},{7,8},{8,9},{9,10},{10,1... | collective-permute-start | bytes 24584 | tf_op jit(solution)/shard_map/ppermute | solution.py:25
  159.3 6.5 %collective-permute-start.1 = (bf16[4,1,64,16]{3,2,1,0:T(8,128)(2,1)S(1)}, bf16[4,1,64,16]{3,2,1,0:T(8,128)(2,1)S(1)}, u32[]{:S(2)}, u32[]{:S(2)}) collective-permute-start(bf16[4,1,64,16]{3,2,1,0:T(8,128)(2,1)S(1)} %get-tuple-element.20), channel_id=1, source_target_pairs={{1,0},{2,1},{3,2},{4,3},{5,4},{6,5},{7,6},{8,7},{9,8},{10,9},{11,1... | collective-permute-start | bytes 24584 | tf_op jit(solution)/shard_map/ppermute | solution.py:27
  167.6 4.6 %copy-start.5 = (bf16[4,2,64,16]{2,3,1,0:T(8,128)(2,1)S(1)}, bf16[4,2,64,16]{2,3,1,0:T(8,128)(2,1)}, u32[]{:S(2)}) copy-start(bf16[4,2,64,16]{2,3,1,0:T(8,128)(2,1)} %get-tuple-element.49) | copy-start | bytes 49156
  174.6 3.6 %copy-start.9 = (f32[512]{0:T(512)S(1)}, f32[512]{0:T(512)}, u32[]{:S(2)}) copy-start(f32[512]{0:T(512)} %param.17) | copy-start | bytes 6148
where the time goes:
time: 182 us; the launch traced here: 180 us
  waiting for transfers between devices  77.6 us (43%)
  local copies, waits for them, and re-layouts  36.9 us (20%)
  starting transfers between devices  31.7 us (17%)
  matrix products  18.4 us (10%)
  blocking collectives  9.28 us (5%)
  other arithmetic  6.04 us (3%)
    all_to_all x1, waiting for transfers between devices, shards(): lax.all_to_all(key_copies, 'seq', split_axis=0, concat_axis=1, tiled=True)  33.1 us
    all_to_all x1, waiting for transfers between devices, shards(): lax.all_to_all(value_copies, 'seq', split_axis=0, concat_axis=1, tiled=True)  18.2 us
    all_to_all x1, waiting for transfers between devices, shards(): lax.all_to_all(result, 'seq', split_axis=1, concat_axis=0, tiled=True)  11.1 us
    all_to_all x1, waiting for transfers between devices, shards(): lax.all_to_all(to_pieces(queries, blocks), 'seq', split_axis=0, concat_ax...  10.7 us
    all_to_all x1, blocking collectives, shards(): tile = lax.all_to_all(laid, 'seq', split_axis=1, concat_axis=0, tiled=True)  9.28 us
    slice x28, local copies, waits for them, and re-layouts, convolve(): padded[shift_t:shift_t + frames, shift_x:shift_x + width, shift_y:shift_y...  8.1 us
    all_to_all x1, starting transfers between devices, shards(): lax.all_to_all(result, 'seq', split_axis=1, concat_axis=0, tiled=True)  7.52 us
    all_to_all x1, starting transfers between devices, shards(): lax.all_to_all(value_copies, 'seq', split_axis=0, concat_axis=1, tiled=True)  7.5 us
  transfers between devices with their start and end apart: 6, of which 5 were waited for; matrix products, arithmetic and copies ran while one was open for 8% of the time, Pallas kernels for 0%

commit v1 on v0

v1 whole, which is shorter than its diff:
```python
import functools
import math

import jax
import jax.numpy as jnp
from jax import lax
from jax.experimental import pallas as pl
from jax.experimental.pallas import tpu as pltpu
from jax.sharding import PartitionSpec as P

HEADS = 12
HEAD_DIM = 128
HEAD_GROUPS = 4
LATENT_CH = 16
FRAMES = 4
ROWS = 32
PER_HEAD = HEADS // HEAD_GROUPS
WIDTH = PER_HEAD * HEAD_DIM
BF = jnp.bfloat16
F32 = jnp.float32


def mm(a, b):
    return lax.dot_general(a, b, (((1,), (0,)), ((), ())), preferred_element_type=F32)


def iota(shape, dim):
    return lax.broadcasted_iota(jnp.int32, shape, dim)


def ones_where(cond):
    return jnp.where(cond, 1.0, 0.0).astype(BF)


def kernel(
    n,
    q_ref, k_ref, v_ref, w_out_hbm, shift_ref, scale_ref, w_final_hbm, conv_w_hbm, bias_ref,
    out_ref,
    qb, kb, vb, m_ref, l_ref, acc_ref, ob, att, w_out_v, w_final_v, conv_v, big_w, proj, send_b, recv_b,
    z_send, z_recv, g_send, g_recv, o_send, o_recv, e_send, e_recv, loc,
):
    me = lax.axis_index("seq")
    blk = n // HEAD_GROUPS
    grp = me // blk
    pos = me % blk
    tok = q_ref.shape[0]
    rows_dev = tok // n
    bits = [1 << i for i in reversed(range(blk.bit_length() - 1))]

    def cols(g):
        return pl.ds(pl.multiple_of(g * WIDTH, 128), WIDTH)

    def remote(src, dst, ssem, rsem, dev):
        return pltpu.make_async_remote_copy(
            src_ref=src, dst_ref=dst, send_sem=ssem, recv_sem=rsem,
            device_id={"seq": dev}, device_id_type=pl.DeviceIdType.MESH,
        )

    barrier = pltpu.get_barrier_semaphore()

    def greet(i, c):
        pl.semaphore_signal(
            barrier, inc=1, device_id={"seq": (me + i) % n}, device_id_type=pl.DeviceIdType.MESH
        )
        return c

    lax.fori_loop(1, n, greet, 0)

    srcs = (q_ref, k_ref, v_ref)
    own = [
        pltpu.make_async_copy(q_ref.at[:, cols(grp)], qb.at[grp], loc.at[0]),
        pltpu.make_async_copy(k_ref.at[:, cols(grp)], kb.at[grp, pos], loc.at[1]),
        pltpu.make_async_copy(v_ref.at[:, cols(grp)], vb.at[grp, pos], loc.at[2]),
    ]
    weights = [
        pltpu.make_async_copy(w_out_hbm, w_out_v, loc.at[3]),
        pltpu.make_async_copy(w_final_hbm, w_final_v, loc.at[4]),
        pltpu.make_async_copy(conv_w_hbm, conv_v, loc.at[5]),
    ]
    for c in own + weights[::-1]:
        c.start()
    pl.semaphore_wait(barrier, n - 1)

    def z_copy(t, j):
        tgt = (grp + j) % HEAD_GROUPS
        dst = (qb.at[grp], kb.at[grp, pos], vb.at[grp, pos])[t]
        return remote(srcs[t].at[:, cols(tgt)], dst, z_send.at[t, j], z_recv.at[t, j], tgt * blk + pos)

    def z_wait(t, j):
        src = (grp + HEAD_GROUPS - j) % HEAD_GROUPS
        dst = (qb.at[src], kb.at[src, pos], vb.at[src, pos])[t]
        remote(dst, dst, z_send.at[t, j], z_recv.at[t, j], src * blk + pos).wait_recv()

    bufs = (None, kb, vb)

    def g_copy(t, j, mask, bit):
        slot = (grp + HEAD_GROUPS - j) % HEAD_GROUPS
        if j == 0 and mask == 0:
            src = srcs[t].at[:, cols(grp)]
        else:
            src = bufs[t].at[slot, pos ^ mask]
        return remote(
            src, bufs[t].at[slot, pos ^ mask],
            g_send.at[t - 1, j, mask | bit], g_recv.at[t - 1, j, mask | bit], grp * blk + (pos ^ bit),
        )

    def g_wait(t, j, mask):
        slot = (grp + HEAD_GROUPS - j) % HEAD_GROUPS
        dst = bufs[t].at[slot, pos ^ mask]
        bit = mask & -mask
        remote(
            dst, dst, g_send.at[t - 1, j, mask], g_recv.at[t - 1, j, mask], grp * blk + (pos ^ bit)
        ).wait_recv()

    sent = []

    def forward(t, j, mask):
        for bit in bits:
            if mask == 0 or bit < (mask & -mask):
                c = g_copy(t, j, mask, bit)
                c.start()
                sent.append(c)

    inner = sorted(range(1, blk), key=lambda m: -(m & -m))

    def gather_rest(j):
        for mask in inner:
            for t in (1, 2):
                g_wait(t, j, mask)
                forward(t, j, mask)

    for j in range(1, HEAD_GROUPS):
        c = z_copy(0, j)
        c.start()
        sent.append(c)
    for t in (1, 2):
        forward(t, 0, 0)
    for j in range(1, HEAD_GROUPS):
        for t in (1, 2):
            c = z_copy(t, j)
            c.start()
            sent.append(c)

    m_ref[...] = jnp.full(m_ref.shape, -1e30, F32)
    l_ref[...] = jnp.zeros(l_ref.shape, F32)
    acc_ref[...] = jnp.zeros(acc_ref.shape, F32)
    weights[2].wait()
    big_w[...] = jnp.zeros(big_w.shape, BF)
    out_ch = conv_v.shape[1]
    for a in range(3):
        for e in range(3):
            for b in range(3):
                for s in range(2):
                    big_w[
                        (a * 3 + e) * 64 + (b + s) * 16 : (a * 3 + e) * 64 + (b + s) * 16 + 16,
                        s * out_ch : (s + 1) * out_ch,
                    ] = conv_v[(9 * a + 3 * b + e) * 16 : (9 * a + 3 * b + e) * 16 + 16, :]

    for c in own:
        c.wait()
    gather_rest(0)
    for j in range(1, HEAD_GROUPS):
        z_wait(0, j)

    queries = HEAD_GROUPS * tok
    part = min(blk, 4)
    factor = math.log2(math.e) / math.sqrt(HEAD_DIM)

    def attend(slot):
        def some(i, c):
            for h in range(PER_HEAD):
                hs = slice(h * HEAD_DIM, (h + 1) * HEAD_DIM)
                qh = qb[:, :, hs].reshape(queries, HEAD_DIM)
                kh = kb[slot, pl.ds(i * part, part), :, hs].reshape(part * tok, HEAD_DIM)
                vh = vb[slot, pl.ds(i * part, part), :, hs].reshape(part * tok, HEAD_DIM)
                s = lax.dot_general(qh, kh, (((1,), (1,)), ((), ())), preferred_element_type=F32)
                s = s * factor
                old = m_ref[h]
                new = jnp.maximum(old, jnp.max(s, axis=1, keepdims=True))
                p = jnp.exp2(s - new)
                alpha = jnp.exp2(old - new)
                l_ref[h] = l_ref[h] * alpha + jnp.sum(p, axis=1, keepdims=True)
                acc_ref[h] = acc_ref[h] * alpha + mm(p.astype(BF), vh)
                m_ref[h] = new
            return c

        lax.fori_loop(0, blk // part, some, 0)

    attend(grp)
    for j in range(1, HEAD_GROUPS):
        for t in (1, 2):
            z_wait(t, j)
            forward(t, j, 0)
        gather_rest(j)
        attend((grp + HEAD_GROUPS - j) % HEAD_GROUPS)

    for h in range(PER_HEAD):
        res = (acc_ref[h] / l_ref[h]).astype(BF)
        ob[:, :, h * HEAD_DIM : (h + 1) * HEAD_DIM] = res.reshape(HEAD_GROUPS, tok, HEAD_DIM)
    for j in range(1, HEAD_GROUPS):
        tgt = (grp + j) % HEAD_GROUPS
        c = remote(ob.at[tgt], att.at[grp], o_send.at[j], o_recv.at[j], tgt * blk + pos)
        c.start()
        sent.append(c)
    weights[0].wait()
    proj[...] = mm(ob[grp], w_out_v[grp])
    for j in range(1, HEAD_GROUPS):
        src = (grp + HEAD_GROUPS - j) % HEAD_GROUPS
        remote(att.at[src], att.at[src], o_send.at[j], o_recv.at[j], src * blk + pos).wait_recv()
        proj[...] += mm(att[src], w_out_v[src])
    projected = proj[...]
    centered = projected - jnp.mean(projected, axis=1, keepdims=True)
    variance = jnp.mean(centered * centered, axis=1, keepdims=True)
    normed = (
        centered * lax.rsqrt(variance + 1e-06) * (1.0 + scale_ref[...]) + shift_ref[...]
    ).astype(BF)
    weights[1].wait()
    patches = mm(normed, w_final_v[...]).astype(BF)

    ch = iota((4 * LATENT_CH, 128), 0)
    lane = iota((4 * LATENT_CH, 128), 1)
    base = 4 * (lane % 16) + 2 * (lane // 64)
    xcol = (lane // 16) % 4
    row = iota((tok, tok), 0)
    col = iota((tok, tok), 1)
    w = row // rows_dev
    here = (row % rows_dev) * n + w
    picks = (
        ((col == here - 1) & (w > 0), (xcol == 0) & (ch == base + 1)),
        ((col == here) & (w == 0), (xcol == 0) & (ch == base)),
        (col == here, ((xcol == 1) & (ch == base)) | ((xcol == 2) & (ch == base + 1))),
        ((col == here + 1) & (w < n - 1), (xcol == 3) & (ch == base)),
        ((col == here) & (w == n - 1), (xcol == 3) & (ch == base + 1)),
    )
    window = None
    for rows_pick, ch_pick in picks:
        term = mm(ones_where(rows_pick), mm(patches, ones_where(ch_pick)).astype(BF))
        window = term if window is None else window + term
    send_b[...] = window.reshape(n, rows_dev, 128)

    def e_copy(i):
        dev = (me + i) % n
        return remote(send_b.at[dev], recv_b.at[me], e_send.at[i], e_recv.at[i], dev)

    def e_start(i, c):
        e_copy(i).start()
        return c

    def e_wait(i, c):
        src = (me + n - i) % n
        remote(recv_b.at[src], recv_b.at[src], e_send.at[i], e_recv.at[i], src).wait_recv()
        e_copy(i).wait_send()
        return c

    lax.fori_loop(1, n, e_start, 0)
    recv_b[me] = send_b[me]
    lax.fori_loop(1, n, e_wait, 0)
    for c in sent:
        c.wait_send()

    got = recv_b[...].reshape(FRAMES * ROWS, 128)
    turned = pltpu.roll(got, 64, 1)
    low = iota(got.shape, 1) < 64
    lo = jnp.concatenate([jnp.where(low, got, 0.0), jnp.where(low, turned, 0.0)], axis=0).astype(BF)
    hi = jnp.concatenate([jnp.where(low, 0.0, turned), jnp.where(low, 0.0, got)], axis=0).astype(BF)
    cells = FRAMES * 2 * ROWS
    orow = iota((cells, cells), 0)
    ocol = iota((cells, cells), 1)
    of = orow // (2 * ROWS)
    oy = orow % (2 * ROWS)

    def pick(idx):
        a, e = idx // 3, idx % 3
        sf = jnp.maximum(of + (a - 2), 0)
        sy = jnp.clip(oy + (e - 1), 0, 2 * ROWS - 1)
        return ones_where(ocol == (sy % 2) * (FRAMES * ROWS) + sf * ROWS + sy // 2)

    feats = []
    for pair in range(5):
        x = mm(pick(2 * pair), lo)
        if 2 * pair + 1 < 9:
            x = x + mm(pick(2 * pair + 1), hi)
        feats.append(x.astype(BF))
    feats = jnp.concatenate(feats, axis=1)
    for s in range(2):
        res = mm(feats, big_w[:, s * out_ch : (s + 1) * out_ch]) + bias_ref[...]
        res = res.astype(BF)
        for f in range(FRAMES):
            out_ref[f, s] = res[f * 2 * ROWS : (f + 1) * 2 * ROWS]


def shards(queries, keys, values, w_out, shift_mod, scale_mod, w_final, conv_weight, conv_bias):
    n = lax.axis_size("seq")
    blk = n // HEAD_GROUPS
    tok = queries.shape[0]
    d = w_out.shape[1]
    out_ch = conv_weight.shape[1]
    vm = pl.BlockSpec(memory_space=pltpu.VMEM)
    hbm = pl.BlockSpec(memory_space=pl.ANY)
    dma = pltpu.SemaphoreType.DMA
    qn = HEAD_GROUPS * tok
    return pl.pallas_call(
        functools.partial(kernel, n),
        out_shape=jax.ShapeDtypeStruct((FRAMES, 2, 2 * ROWS, out_ch), BF),
        in_specs=[vm, vm, vm, hbm, vm, vm, hbm, hbm, vm],
        out_specs=vm,
        scratch_shapes=[
            pltpu.VMEM((HEAD_GROUPS, tok, WIDTH), BF),
            pltpu.VMEM((HEAD_GROUPS, blk, tok, WIDTH), BF),
            pltpu.VMEM((HEAD_GROUPS, blk, tok, WIDTH), BF),
            pltpu.VMEM((PER_HEAD, qn, 1), F32),
            pltpu.VMEM((PER_HEAD, qn, 1), F32),
            pltpu.VMEM((PER_HEAD, qn, HEAD_DIM), F32),
            pltpu.VMEM((HEAD_GROUPS, tok, WIDTH), BF),
            pltpu.VMEM((HEAD_GROUPS, tok, WIDTH), BF),
            pltpu.VMEM((HEAD_GROUPS, WIDTH, d), BF),
            pltpu.VMEM(w_final.shape, BF),
            pltpu.VMEM(conv_weight.shape, BF),
            pltpu.VMEM((640, 2 * out_ch), BF),
            pltpu.VMEM((tok, d), F32),
            pltpu.VMEM((n, tok // n, 128), F32),
            pltpu.VMEM((n, tok // n, 128), F32),
            dma((3, HEAD_GROUPS)), dma((3, HEAD_GROUPS)),
            dma((2, HEAD_GROUPS, blk)), dma((2, HEAD_GROUPS, blk)),
            dma((HEAD_GROUPS,)), dma((HEAD_GROUPS,)),
            dma((n,)), dma((n,)),
            dma((6,)),
        ],
        compiler_params=pltpu.CompilerParams(
            collective_id=0, has_side_effects=True, vmem_limit_bytes=60 * 1024 * 1024
        ),
        name="fused",
    )(
        queries, keys, values, w_out.reshape(HEAD_GROUPS, WIDTH, d),
        shift_mod.reshape(1, d), scale_mod.reshape(1, d), w_final, conv_weight,
        conv_bias.reshape(1, out_ch),
    )


def solution(mesh):
    placed = (
        P(("groups", "seq"), None),
        P(("groups", "seq"), None),
        P(("groups", "seq"), None),
        P(),
        P("groups"),
        P("groups"),
        P(),
        P(),
        P(),
    )
    return jax.shard_map(
        shards,
        mesh=mesh,
        in_specs=placed,
        out_specs=P("groups", "seq", None, None),
        check_vma=False,
    )
```

time: 182 us -> 84.7 us (0.47)
  the two profiles are of different devices: /device:TPU:3 before, /device:TPU:0 now
where the time goes in v1:
time: 84.7 us; the launch traced here: 84.5 us
  Pallas kernels  80.4 us (95%)
  local copies, waits for them, and re-layouts  4.02 us (5%)
    pallas_call x1, Pallas kernels, shards(): pl.pallas_call(functools.partial(kernel, n), out_shape=jax.ShapeDtypeStru...  80.4 us
    unnamed x2, local copies, waits for them, and re-layouts  4.02 us

profile of v1, /device:TPU:0, one launch (start us, length us, event | category | flops | bytes accessed | tf_op | source)
XLA Modules:
  0.0 84.5 jit_solution(14006845028442898917)
XLA Ops:
  0.0 2.1 %copy.10.w_final_hbm = bf16[3072,64]{1,0:T(8,128)(2,1)} copy(bf16[3072,64]{0,1:T(8,128)(2,1)} %param.15) | data formatting | bytes 786432 | tf_op args[6]
  2.1 80.4 %fused.1 = bf16[4,2,64,512]{3,2,1,0:T(8,128)(2,1)} custom-call(bf16[128,1536]{1,0:T(8,128)(2,1)} %q_ref.1, bf16[128,1536]{1,0:T(8,128)(2,1)} %k_ref.1, bf16[128,1536]{1,0:T(8,128)(2,1)} %v_ref.1, bf16[4,384,3072]{2,1,0:T(8,128)(2,1)} %bitcast.4, f32[1,3072]{1,0:T(1,128)} %bitcast.5, f32[1,3072]{1,0:T(1,128)} %bitcast.6, bf16[3072,64]{1,0:T(8,128)(2,1)} %copy.10.w_final_hbm, ...), custom_call_target="tpu_custom_call" | custom-call | tf_op jit(solution)/shard_map/fused/pallas_call | solution.py:302
  82.6 1.9 %copy.12 = bf16[4,2,64,512]{3,2,1,0:T(8,128)(2,1)} copy(bf16[4,2,64,512]{3,2,1,0:T(8,128)(2,1)} %fused.1) | data formatting | bytes 1048576

commit v2 on v1

v2 whole, which is shorter than its diff:
```python
import functools
import math

import jax
import jax.numpy as jnp
from jax import lax
from jax.experimental import pallas as pl
from jax.experimental.pallas import tpu as pltpu
from jax.sharding import PartitionSpec as P

HEADS = 12
HEAD_DIM = 128
HEAD_GROUPS = 4
LATENT_CH = 16
FRAMES = 4
ROWS = 32
PER_HEAD = HEADS // HEAD_GROUPS
WIDTH = PER_HEAD * HEAD_DIM
BF = jnp.bfloat16
F32 = jnp.float32


def mm(a, b):
    return lax.dot_general(a, b, (((1,), (0,)), ((), ())), preferred_element_type=F32)


def iota(shape, dim):
    return lax.broadcasted_iota(jnp.int32, shape, dim)


def ones_where(cond):
    return jnp.where(cond, 1.0, 0.0).astype(BF)


def kernel(
    n,
    q_ref, k_ref, v_ref, w_out_hbm, shift_ref, scale_ref, w_final_hbm,
    out_ref,
    qb, kb, vb, m_ref, l_ref, acc_ref, ob, att, w_out_v, w_final_v, proj, send_b, recv_b,
    z_send, z_recv, g_send, g_recv, o_send, o_recv, e_send, e_recv, loc,
):
    me = lax.axis_index("seq")
    blk = n // HEAD_GROUPS
    grp = me // blk
    pos = me % blk
    tok = q_ref.shape[0]
    rows_dev = tok // n
    bits = [1 << i for i in reversed(range(blk.bit_length() - 1))]

    def cols(g, h):
        return pl.ds(pl.multiple_of(g * WIDTH + h * HEAD_DIM, 128), HEAD_DIM)

    def remote(src, dst, ssem, rsem, dev):
        return pltpu.make_async_remote_copy(
            src_ref=src, dst_ref=dst, send_sem=ssem, recv_sem=rsem,
            device_id={"seq": dev}, device_id_type=pl.DeviceIdType.MESH,
        )

    barrier = pltpu.get_barrier_semaphore()

    def greet(i, c):
        pl.semaphore_signal(
            barrier, inc=1, device_id={"seq": (me + i) % n}, device_id_type=pl.DeviceIdType.MESH
        )
        return c

    lax.fori_loop(1, n, greet, 0)

    srcs = (q_ref, k_ref, v_ref)
    bufs = (qb, kb, vb)

    def home(t, h, slot):
        return qb.at[h, slot] if t == 0 else bufs[t].at[h, slot, pos]

    own = [
        pltpu.make_async_copy(srcs[t].at[:, cols(grp, h)], home(t, h, grp), loc.at[h * 3 + t])
        for h in range(PER_HEAD)
        for t in range(3)
    ]
    w_out_copies = [
        pltpu.make_async_copy(w_out_hbm.at[:, h], w_out_v.at[h], loc.at[9 + h]) for h in range(PER_HEAD)
    ]
    w_final_copy = pltpu.make_async_copy(w_final_hbm, w_final_v, loc.at[12])
    for c in own + w_out_copies + [w_final_copy]:
        c.start()
    pl.semaphore_wait(barrier, n - 1)

    def slot_of(j):
        return (grp + HEAD_GROUPS - j) % HEAD_GROUPS

    sent = []

    def z_start(t, h, j):
        tgt = (grp + j) % HEAD_GROUPS
        c = remote(
            srcs[t].at[:, cols(tgt, h)], home(t, h, grp),
            z_send.at[t, h, j], z_recv.at[t, h, j], tgt * blk + pos,
        )
        c.start()
        sent.append(c)

    def z_wait(t, h, j):
        dst = home(t, h, slot_of(j))
        remote(dst, dst, z_send.at[t, h, j], z_recv.at[t, h, j], slot_of(j) * blk + pos).wait_recv()

    def g_copy(t, h, j, mask, bit, src=None):
        dst = bufs[t].at[h, slot_of(j), pos ^ mask]
        return remote(
            dst if src is None else src, dst,
            g_send.at[t - 1, h, j, mask + bit], g_recv.at[t - 1, h, j, mask + bit],
            grp * blk + (pos ^ bit),
        )

    def g_wait(t, h, j, mask, bit):
        dst = bufs[t].at[h, slot_of(j), pos ^ mask]
        remote(
            dst, dst, g_send.at[t - 1, h, j, mask], g_recv.at[t - 1, h, j, mask], grp * blk + (pos ^ bit)
        ).wait_recv()

    def first(h, j):
        for t in (1, 2):
            if j:
                z_wait(t, h, j)
            for bit in bits:
                g_copy(t, h, j, 0, bit, None if j else srcs[t].at[:, cols(grp, h)]).start()

    def relay(h, j, some_bits):
        for bit in some_bits:

            def one(i, c):
                mask = bit + i * (2 * bit)
                for t in (1, 2):
                    g_wait(t, h, j, mask, bit)
                    for low in bits:
                        if low < bit:
                            g_copy(t, h, j, mask, low).start()
                return c

            lax.fori_loop(0, blk // (2 * bit), one, 0)

    for h in range(PER_HEAD):
        for j in range(1, HEAD_GROUPS):
            z_start(0, h, j)
        if h == 0:
            first(0, 0)
        for j in range(1, HEAD_GROUPS):
            for t in (1, 2):
                z_start(t, h, j)

    m_ref[...] = jnp.full(m_ref.shape, -1e30, F32)
    l_ref[...] = jnp.zeros(l_ref.shape, F32)
    acc_ref[...] = jnp.zeros(acc_ref.shape, F32)
    for c in own:
        c.wait()

    queries = HEAD_GROUPS * tok
    part = min(blk, 4)
    factor = math.log2(math.e) / math.sqrt(HEAD_DIM)

    def attend(h, slot):
        def some(i, c):
            qh = qb[h].reshape(queries, HEAD_DIM)
            kh = kb[h, slot, pl.ds(i * part, part)].reshape(part * tok, HEAD_DIM)
            vh = vb[h, slot, pl.ds(i * part, part)].reshape(part * tok, HEAD_DIM)
            s = lax.dot_general(qh, kh, (((1,), (1,)), ((), ())), preferred_element_type=F32)
            s = s * factor
            old = m_ref[h]
            new = jnp.maximum(old, jnp.max(s, axis=1, keepdims=True))
            p = jnp.exp2(s - new)
            alpha = jnp.exp2(old - new)
            l_ref[h] = l_ref[h] * alpha + jnp.sum(p, axis=1, keepdims=True)
            acc_ref[h] = acc_ref[h] * alpha + mm(p.astype(BF), vh)
            m_ref[h] = new
            return c

        lax.fori_loop(0, blk // part, some, 0)

    def finish(h):
        ob[h] = (acc_ref[h] / l_ref[h]).astype(BF).reshape(HEAD_GROUPS, tok, HEAD_DIM)
        lanes = pl.ds(pl.multiple_of(grp * HEAD_DIM, 128), HEAD_DIM)
        for j in range(1, HEAD_GROUPS):
            tgt = (grp + j) % HEAD_GROUPS
            c = remote(
                ob.at[h, tgt], att.at[h, :, lanes], o_send.at[h, j], o_recv.at[h, j], tgt * blk + pos
            )
            c.start()
            sent.append(c)
        att[h, :, lanes] = ob[h, grp]

    units = [(h, j) for h in range(PER_HEAD) for j in range(HEAD_GROUPS)]
    count = len(units)
    for u in range(-2, count):
        if 0 <= u + 2 < count and u + 2 > 0:
            first(*units[u + 2])
        if 0 <= u + 1 < count:
            relay(*units[u + 1], bits[:-1])
        if u >= 0:
            h, j = units[u]
            relay(h, j, bits[-1:])
            if j == 0:
                for i in range(1, HEAD_GROUPS):
                    z_wait(0, h, i)
            attend(h, slot_of(j))
            if j == HEAD_GROUPS - 1:
                finish(h)

    for h in range(PER_HEAD):
        w_out_copies[h].wait()
        for j in range(1, HEAD_GROUPS):
            lanes = pl.ds(pl.multiple_of(slot_of(j) * HEAD_DIM, 128), HEAD_DIM)
            dst = att.at[h, :, lanes]
            remote(dst, dst, o_send.at[h, j], o_recv.at[h, j], slot_of(j) * blk + pos).wait_recv()
        term = mm(att[h], w_out_v[h].reshape(HEAD_GROUPS * HEAD_DIM, proj.shape[1]))
        proj[...] = term if h == 0 else proj[...] + term
    projected = proj[...]
    centered = projected - jnp.mean(projected, axis=1, keepdims=True)
    variance = jnp.mean(centered * centered, axis=1, keepdims=True)
    normed = (
        centered * lax.rsqrt(variance + 1e-06) * (1.0 + scale_ref[...]) + shift_ref[...]
    ).astype(BF)
    w_final_copy.wait()
    patches = lax.dot_general(
        normed, w_final_v[...], (((1,), (1,)), ((), ())), preferred_element_type=F32
    ).astype(BF)

    ch = iota((4 * LATENT_CH, 128), 0)
    lane = iota((4 * LATENT_CH, 128), 1)
    base = 4 * (lane % 16) + 2 * (lane // 64)
    xcol = (lane // 16) % 4
    row = iota((tok, tok), 0)
    col = iota((tok, tok), 1)
    w = row // rows_dev
    here = (row % rows_dev) * n + w
    picks = (
        ((col == here - 1) & (w > 0), (xcol == 0) & (ch == base + 1)),
        ((col == here) & (w == 0), (xcol == 0) & (ch == base)),
        (col == here, ((xcol == 1) & (ch == base)) | ((xcol == 2) & (ch == base + 1))),
        ((col == here + 1) & (w < n - 1), (xcol == 3) & (ch == base)),
        ((col == here) & (w == n - 1), (xcol == 3) & (ch == base + 1)),
    )
    window = None
    for rows_pick, ch_pick in picks:
        term = mm(ones_where(rows_pick), mm(patches, ones_where(ch_pick)).astype(BF))
        window = term if window is None else window + term
    send_b[...] = window.reshape(n, rows_dev, 128)

    def e_copy(i):
        dev = (me + i) % n
        return remote(send_b.at[dev], recv_b.at[me], e_send.at[i], e_recv.at[i], dev)

    def e_start(i, c):
        e_copy(i).start()
        return c

    def e_wait(i, c):
        src = (me + n - i) % n
        remote(recv_b.at[src], recv_b.at[src], e_send.at[i], e_recv.at[i], src).wait_recv()
        e_copy(i).wait_send()
        return c

    lax.fori_loop(1, n, e_start, 0)
    recv_b[me] = send_b[me]
    lax.fori_loop(1, n, e_wait, 0)
    for c in sent:
        c.wait_send()

    def drain(i, c):
        h = i // (HEAD_GROUPS * (blk - 1))
        j = (i // (blk - 1)) % HEAD_GROUPS
        mask = i % (blk - 1) + 1
        for t in (1, 2):
            ref = bufs[t].at[0, 0, 0]
            remote(
                ref, ref, g_send.at[t - 1, h, j, mask], g_recv.at[t - 1, h, j, mask], (me + 1) % n
            ).wait_send()
        return c

    lax.fori_loop(0, PER_HEAD * HEAD_GROUPS * (blk - 1), drain, 0)
    out_ref[...] = recv_b[...].reshape(out_ref.shape)


def conv_kernel(got_ref, conv_v, bias_ref, out_ref, big_w):
    out_ch = conv_v.shape[1]
    big_w[...] = jnp.zeros(big_w.shape, BF)
    for a in range(3):
        for e in range(3):
            for b in range(3):
                for s in range(2):
                    big_w[
                        (a * 3 + e) * 64 + (b + s) * 16 : (a * 3 + e) * 64 + (b + s) * 16 + 16,
                        s * out_ch : (s + 1) * out_ch,
                    ] = conv_v[(9 * a + 3 * b + e) * 16 : (9 * a + 3 * b + e) * 16 + 16, :]
    got = got_ref[...]
    turned = pltpu.roll(got, 64, 1)
    low = iota(got.shape, 1) < 64
    lo = jnp.concatenate([jnp.where(low, got, 0.0), jnp.where(low, turned, 0.0)], axis=0).astype(BF)
    hi = jnp.concatenate([jnp.where(low, 0.0, turned), jnp.where(low, 0.0, got)], axis=0).astype(BF)
    cells = FRAMES * 2 * ROWS
    orow = iota((cells, cells), 0)
    ocol = iota((cells, cells), 1)
    of = orow // (2 * ROWS)
    oy = orow % (2 * ROWS)

    def pick(idx):
        a, e = idx // 3, idx % 3
        sf = jnp.maximum(of + (a - 2), 0)
        sy = jnp.clip(oy + (e - 1), 0, 2 * ROWS - 1)
        return ones_where(ocol == (sy % 2) * (FRAMES * ROWS) + sf * ROWS + sy // 2)

    feats = []
    for pair in range(5):
        x = mm(pick(2 * pair), lo)
        if 2 * pair + 1 < 9:
            x = x + mm(pick(2 * pair + 1), hi)
        feats.append(x.astype(BF))
    feats = jnp.concatenate(feats, axis=1)
    for s in range(2):
        res = mm(feats, big_w[:, s * out_ch : (s + 1) * out_ch]) + bias_ref[...]
        res = res.astype(BF)
        for f in range(FRAMES):
            out_ref[f, s] = res[f * 2 * ROWS : (f + 1) * 2 * ROWS]

def shards(queries, keys, values, w_out, shift_mod, scale_mod, w_final, conv_weight, conv_bias):
    n = lax.axis_size("seq")
    blk = n // HEAD_GROUPS
    tok = queries.shape[0]
    d = w_out.shape[1]
    out_ch = conv_weight.shape[1]
    vm = pl.BlockSpec(memory_space=pltpu.VMEM)
    hbm = pl.BlockSpec(memory_space=pl.ANY)
    dma = pltpu.SemaphoreType.DMA
    qn = HEAD_GROUPS * tok
    got = pl.pallas_call(
        functools.partial(kernel, n),
        out_shape=jax.ShapeDtypeStruct((FRAMES * ROWS, 128), F32),
        in_specs=[vm, vm, vm, hbm, vm, vm, hbm],
        out_specs=vm,
        scratch_shapes=[
            pltpu.VMEM((PER_HEAD, HEAD_GROUPS, tok, HEAD_DIM), BF),
            pltpu.VMEM((PER_HEAD, HEAD_GROUPS, blk, tok, HEAD_DIM), BF),
            pltpu.VMEM((PER_HEAD, HEAD_GROUPS, blk, tok, HEAD_DIM), BF),
            pltpu.VMEM((PER_HEAD, qn, 1), F32),
            pltpu.VMEM((PER_HEAD, qn, 1), F32),
            pltpu.VMEM((PER_HEAD, qn, HEAD_DIM), F32),
            pltpu.VMEM((PER_HEAD, HEAD_GROUPS, tok, HEAD_DIM), BF),
            pltpu.VMEM((PER_HEAD, tok, HEAD_GROUPS * HEAD_DIM), BF),
            pltpu.VMEM((PER_HEAD, HEAD_GROUPS, HEAD_DIM, d), BF),
            pltpu.VMEM(w_final.shape[::-1], BF),
            pltpu.VMEM((tok, d), F32),
            pltpu.VMEM((n, tok // n, 128), F32),
            pltpu.VMEM((n, tok // n, 128), F32),
            dma((3, PER_HEAD, HEAD_GROUPS)), dma((3, PER_HEAD, HEAD_GROUPS)),
            dma((2, PER_HEAD, HEAD_GROUPS, blk)), dma((2, PER_HEAD, HEAD_GROUPS, blk)),
            dma((PER_HEAD, HEAD_GROUPS)), dma((PER_HEAD, HEAD_GROUPS)),
            dma((n,)), dma((n,)),
            dma((13,)),
        ],
        compiler_params=pltpu.CompilerParams(
            collective_id=0, has_side_effects=True, vmem_limit_bytes=56 * 1024 * 1024
        ),
        name="fused",
    )(
        queries, keys, values, w_out.reshape(HEAD_GROUPS, PER_HEAD, HEAD_DIM, d),
        shift_mod.reshape(1, d), scale_mod.reshape(1, d), w_final.T,
    )
    return pl.pallas_call(
        conv_kernel,
        out_shape=jax.ShapeDtypeStruct((FRAMES, 2, 2 * ROWS, out_ch), BF),
        in_specs=[vm, vm, vm],
        out_specs=vm,
        scratch_shapes=[pltpu.VMEM((640, 2 * out_ch), BF)],
        name="conv",
    )(got, conv_weight, conv_bias.reshape(1, out_ch))


def solution(mesh):
    placed = (
        P(("groups", "seq"), None),
        P(("groups", "seq"), None),
        P(("groups", "seq"), None),
        P(),
        P("groups"),
        P("groups"),
        P(),
        P(),
        P(),
    )
    return jax.shard_map(
        shards,
        mesh=mesh,
        in_specs=placed,
        out_specs=P("groups", "seq", None, None),
        check_vma=False,
    )
```

time: 84.7 us -> 67 us (0.79)
  Pallas kernels: 80.4 us -> 66.8 us
  local copies, waits for them, and re-layouts: 4.02 us -> 0 us
    pallas_call x1, Pallas kernels: 80.4 us -> 64 us  [shards(): pl.pallas_call(functools.partial(kernel, n), out_shape=jax.ShapeDtypeStru...]
    unnamed x2 -> x0, local copies, waits for them, and re-layouts: 4.02 us -> none
    pallas_call x0 -> x1, Pallas kernels: none -> 2.8 us  [shards(): pl.pallas_call(conv_kernel, out_shape=jax.ShapeDtypeStruct((FRAMES, 2, 2...]
where the time goes in v2:
time: 67 us; the launch traced here: 66.8 us
  Pallas kernels  66.8 us (100%)
    pallas_call x1, Pallas kernels, shards(): pl.pallas_call(functools.partial(kernel, n), out_shape=jax.ShapeDtypeStru...  64 us
    pallas_call x1, Pallas kernels, shards(): pl.pallas_call(conv_kernel, out_shape=jax.ShapeDtypeStruct((FRAMES, 2, 2...  2.8 us

profile of v2, /device:TPU:0, one launch (start us, length us, event | category | flops | bytes accessed | tf_op | source)
XLA Modules:
  0.0 66.8 jit_solution(17353804453274076168)
XLA Ops:
  0.0 64.0 %fused.1.got_ref = f32[128,128]{1,0:T(8,128)} custom-call(bf16[128,1536]{1,0:T(8,128)(2,1)} %q_ref.1, bf16[128,1536]{1,0:T(8,128)(2,1)} %k_ref.1, bf16[128,1536]{1,0:T(8,128)(2,1)} %v_ref.1, bf16[4,3,128,3072]{3,2,1,0:T(8,128)(2,1)} %bitcast.5, f32[1,3072]{1,0:T(1,128)} %bitcast.7, f32[1,3072]{1,0:T(1,128)} %bitcast.8, bf16[64,3072]{1,0:T(8,128)(2,1)} %bitcast.6), custom_call_target="tpu_custom_call" | custom-call | tf_op jit(solution)/shard_map/fused/pallas_call | solution.py:333
  64.0 2.8 %conv.1 = bf16[4,2,64,512]{3,2,1,0:T(8,128)(2,1)} custom-call(f32[128,128]{1,0:T(8,128)} %fused.1.got_ref, bf16[432,512]{1,0:T(8,128)(2,1)} %conv_v.1, f32[1,512]{1,0:T(1,128)} %bitcast.9), custom_call_target="tpu_custom_call" | custom-call | tf_op jit(solution)/shard_map/conv/pallas_call | solution.py:366

commit v3 on v2

--- a/solution.py
+++ b/solution.py
@@ -34,16 +34,16 @@
 
 def kernel(
     n,
-    q_ref, k_ref, v_ref, w_out_hbm, shift_ref, scale_ref, w_final_hbm,
+    q_hbm, k_hbm, v_hbm, w_out_hbm, shift_ref, scale_ref, w_final_hbm,
     out_ref,
-    qb, kb, vb, m_ref, l_ref, acc_ref, ob, att, w_out_v, w_final_v, proj, send_b, recv_b,
+    q_ref, k_ref, v_ref, qb, kb, vb, m_ref, acc_ref, ob, att, w_out_v, w_final_v, proj, send_b, recv_b,
     z_send, z_recv, g_send, g_recv, o_send, o_recv, e_send, e_recv, loc,
 ):
     me = lax.axis_index("seq")
     blk = n // HEAD_GROUPS
     grp = me // blk
     pos = me % blk
-    tok = q_ref.shape[0]
+    tok = q_hbm.shape[0]
     rows_dev = tok // n
     bits = [1 << i for i in reversed(range(blk.bit_length() - 1))]
 
@@ -66,14 +66,16 @@
 
     lax.fori_loop(1, n, greet, 0)
 
+    raw = (q_hbm, k_hbm, v_hbm)
     srcs = (q_ref, k_ref, v_ref)
+    staged = [pltpu.make_async_copy(raw[t], srcs[t], loc.at[13 + t]) for t in range(3)]
     bufs = (qb, kb, vb)
 
     def home(t, h, slot):
         return qb.at[h, slot] if t == 0 else bufs[t].at[h, slot, pos]
 
     own = [
-        pltpu.make_async_copy(srcs[t].at[:, cols(grp, h)], home(t, h, grp), loc.at[h * 3 + t])
+        pltpu.make_async_copy(raw[t].at[:, cols(grp, h)], home(t, h, grp), loc.at[h * 3 + t])
         for h in range(PER_HEAD)
         for t in range(3)
     ]
@@ -81,9 +83,11 @@
         pltpu.make_async_copy(w_out_hbm.at[:, h], w_out_v.at[h], loc.at[9 + h]) for h in range(PER_HEAD)
     ]
     w_final_copy = pltpu.make_async_copy(w_final_hbm, w_final_v, loc.at[12])
-    for c in own + w_out_copies + [w_final_copy]:
+    for c in staged + own + w_out_copies + [w_final_copy]:
         c.start()
     pl.semaphore_wait(barrier, n - 1)
+    for c in staged:
+        c.wait()
 
     def slot_of(j):
         return (grp + HEAD_GROUPS - j) % HEAD_GROUPS
@@ -148,13 +152,13 @@
                 z_start(t, h, j)
 
     m_ref[...] = jnp.full(m_ref.shape, -1e30, F32)
-    l_ref[...] = jnp.zeros(l_ref.shape, F32)
     acc_ref[...] = jnp.zeros(acc_ref.shape, F32)
     for c in own:
         c.wait()
 
     queries = HEAD_GROUPS * tok
     part = min(blk, 4)
+    ones = jnp.ones((part * tok, HEAD_DIM), BF)
     factor = math.log2(math.e) / math.sqrt(HEAD_DIM)
 
     def attend(h, slot):
@@ -168,15 +172,14 @@
             new = jnp.maximum(old, jnp.max(s, axis=1, keepdims=True))
             p = jnp.exp2(s - new)
             alpha = jnp.exp2(old - new)
-            l_ref[h] = l_ref[h] * alpha + jnp.sum(p, axis=1, keepdims=True)
-            acc_ref[h] = acc_ref[h] * alpha + mm(p.astype(BF), vh)
+            acc_ref[h] = acc_ref[h] * alpha + mm(p.astype(BF), jnp.concatenate([vh, ones], axis=1))
             m_ref[h] = new
             return c
 
         lax.fori_loop(0, blk // part, some, 0)
 
     def finish(h):
-        ob[h] = (acc_ref[h] / l_ref[h]).astype(BF).reshape(HEAD_GROUPS, tok, HEAD_DIM)
+        ob[h] = (acc_ref[h, :, :HEAD_DIM] / acc_ref[h, :, HEAD_DIM:]).astype(BF).reshape(HEAD_GROUPS, tok, HEAD_DIM)
         lanes = pl.ds(pl.multiple_of(grp * HEAD_DIM, 128), HEAD_DIM)
         for j in range(1, HEAD_GROUPS):
             tgt = (grp + j) % HEAD_GROUPS
@@ -333,15 +336,17 @@
     got = pl.pallas_call(
         functools.partial(kernel, n),
         out_shape=jax.ShapeDtypeStruct((FRAMES * ROWS, 128), F32),
-        in_specs=[vm, vm, vm, hbm, vm, vm, hbm],
+        in_specs=[hbm, hbm, hbm, hbm, vm, vm, hbm],
         out_specs=vm,
         scratch_shapes=[
+            pltpu.VMEM(queries.shape, BF),
+            pltpu.VMEM(keys.shape, BF),
+            pltpu.VMEM(values.shape, BF),
             pltpu.VMEM((PER_HEAD, HEAD_GROUPS, tok, HEAD_DIM), BF),
             pltpu.VMEM((PER_HEAD, HEAD_GROUPS, blk, tok, HEAD_DIM), BF),
             pltpu.VMEM((PER_HEAD, HEAD_GROUPS, blk, tok, HEAD_DIM), BF),
             pltpu.VMEM((PER_HEAD, qn, 1), F32),
-            pltpu.VMEM((PER_HEAD, qn, 1), F32),
-            pltpu.VMEM((PER_HEAD, qn, HEAD_DIM), F32),
+            pltpu.VMEM((PER_HEAD, qn, 2 * HEAD_DIM), F32),
             pltpu.VMEM((PER_HEAD, HEAD_GROUPS, tok, HEAD_DIM), BF),
             pltpu.VMEM((PER_HEAD, tok, HEAD_GROUPS * HEAD_DIM), BF),
             pltpu.VMEM((PER_HEAD, HEAD_GROUPS, HEAD_DIM, d), BF),
@@ -353,7 +358,7 @@
             dma((2, PER_HEAD, HEAD_GROUPS, blk)), dma((2, PER_HEAD, HEAD_GROUPS, blk)),
             dma((PER_HEAD, HEAD_GROUPS)), dma((PER_HEAD, HEAD_GROUPS)),
             dma((n,)), dma((n,)),
-            dma((13,)),
+            dma((16,)),
         ],
         compiler_params=pltpu.CompilerParams(
             collective_id=0, has_side_effects=True, vmem_limit_bytes=56 * 1024 * 1024

time: 67 us -> 65.3 us (0.975)
  Pallas kernels: 66.8 us -> 65 us
    pallas_call x1, Pallas kernels: 64 us -> 62.2 us  [shards(): pl.pallas_call(functools.partial(kernel, n), out_shape=jax.ShapeDtypeStru...]
where the time goes in v3:
time: 65.3 us; the launch traced here: 65 us
  Pallas kernels  65 us (100%)
    pallas_call x1, Pallas kernels, shards(): pl.pallas_call(functools.partial(kernel, n), out_shape=jax.ShapeDtypeStru...  62.2 us
    pallas_call x1, Pallas kernels, shards(): pl.pallas_call(conv_kernel, out_shape=jax.ShapeDtypeStruct((FRAMES, 2, 2...  2.8 us

profile of v3, /device:TPU:0, one launch (start us, length us, event | category | flops | bytes accessed | tf_op | source)
XLA Modules:
  0.0 65.0 jit_solution(13565536408057089470)
XLA Ops:
  0.0 62.2 %fused.1.got_ref = f32[128,128]{1,0:T(8,128)} custom-call(bf16[128,1536]{1,0:T(8,128)(2,1)} %q_hbm.1, bf16[128,1536]{1,0:T(8,128)(2,1)} %k_hbm.1, bf16[128,1536]{1,0:T(8,128)(2,1)} %v_hbm.1, bf16[4,3,128,3072]{3,2,1,0:T(8,128)(2,1)} %bitcast.5, f32[1,3072]{1,0:T(1,128)} %bitcast.7, f32[1,3072]{1,0:T(1,128)} %bitcast.8, bf16[64,3072]{1,0:T(8,128)(2,1)} %bitcast.6), custom_call_target="tpu_custom_call" | custom-call | tf_op jit(solution)/shard_map/fused/pallas_call | solution.py:336
  62.2 2.8 %conv.1 = bf16[4,2,64,512]{3,2,1,0:T(8,128)(2,1)} custom-call(f32[128,128]{1,0:T(8,128)} %fused.1.got_ref, bf16[432,512]{1,0:T(8,128)(2,1)} %conv_v.1, f32[1,512]{1,0:T(1,128)} %bitcast.9), custom_call_target="tpu_custom_call" | custom-call | tf_op jit(solution)/shard_map/conv/pallas_call | solution.py:371

commit v4 on v3

--- a/solution.py
+++ b/solution.py
@@ -142,12 +142,13 @@
 
             lax.fori_loop(0, blk // (2 * bit), one, 0)
 
+    order = (0, 2, 1, 3)
     for h in range(PER_HEAD):
-        for j in range(1, HEAD_GROUPS):
+        for j in order[1:]:
             z_start(0, h, j)
         if h == 0:
             first(0, 0)
-        for j in range(1, HEAD_GROUPS):
+        for j in order[1:]:
             for t in (1, 2):
                 z_start(t, h, j)
 
@@ -190,7 +191,7 @@
             sent.append(c)
         att[h, :, lanes] = ob[h, grp]
 
-    units = [(h, j) for h in range(PER_HEAD) for j in range(HEAD_GROUPS)]
+    units = [(h, j) for h in range(PER_HEAD) for j in order]
     count = len(units)
     for u in range(-2, count):
         if 0 <= u + 2 < count and u + 2 > 0:
@@ -204,7 +205,7 @@
                 for i in range(1, HEAD_GROUPS):
                     z_wait(0, h, i)
             attend(h, slot_of(j))
-            if j == HEAD_GROUPS - 1:
+            if j == order[-1]:
                 finish(h)
 
     for h in range(PER_HEAD):

time: 65.3 us -> 66.3 us (1.015)
  Pallas kernels: 65 us -> 66 us
    pallas_call x1, Pallas kernels: 62.2 us -> 63.2 us  [shards(): pl.pallas_call(functools.partial(kernel, n), out_shape=jax.ShapeDtypeStru...]
where the time goes in v4:
time: 66.3 us; the launch traced here: 66 us
  Pallas kernels  66 us (100%)
    pallas_call x1, Pallas kernels, shards(): pl.pallas_call(functools.partial(kernel, n), out_shape=jax.ShapeDtypeStru...  63.2 us
    pallas_call x1, Pallas kernels, shards(): pl.pallas_call(conv_kernel, out_shape=jax.ShapeDtypeStruct((FRAMES, 2, 2...  2.8 us

profile of v4, /device:TPU:0, one launch (start us, length us, event | category | flops | bytes accessed | tf_op | source)
XLA Modules:
  0.0 66.0 jit_solution(378842186819575686)
XLA Ops:
  0.0 63.2 %fused.1.got_ref = f32[128,128]{1,0:T(8,128)} custom-call(bf16[128,1536]{1,0:T(8,128)(2,1)} %q_hbm.1, bf16[128,1536]{1,0:T(8,128)(2,1)} %k_hbm.1, bf16[128,1536]{1,0:T(8,128)(2,1)} %v_hbm.1, bf16[4,3,128,3072]{3,2,1,0:T(8,128)(2,1)} %bitcast.5, f32[1,3072]{1,0:T(1,128)} %bitcast.7, f32[1,3072]{1,0:T(1,128)} %bitcast.8, bf16[64,3072]{1,0:T(8,128)(2,1)} %bitcast.6), custom_call_target="tpu_custom_call" | custom-call | tf_op jit(solution)/shard_map/fused/pallas_call | solution.py:337
  63.2 2.8 %conv.1 = bf16[4,2,64,512]{3,2,1,0:T(8,128)(2,1)} custom-call(f32[128,128]{1,0:T(8,128)} %fused.1.got_ref, bf16[432,512]{1,0:T(8,128)(2,1)} %conv_v.1, f32[1,512]{1,0:T(1,128)} %bitcast.9), custom_call_target="tpu_custom_call" | custom-call | tf_op jit(solution)/shard_map/conv/pallas_call | solution.py:372
